TPU v7x, 256 devices: a whole 4x4x8 slice. The times are simulated.
256 devices in a mesh: ctx: 32 (over y, z), head: 8 (over x, core).
Axes of the slice: x: 4, y: 4, z: 8, core: 2. Of those that a mesh axis runs over, the one named last changes fastest.
Arguments:
- lin_q: bfloat16 [4096, 32, 128], P('ctx', 'head'), may hold values from -4 to 4
- lin_k: bfloat16 [4096, 32, 128], P('ctx', 'head'), may hold values from -4 to 4
- lin_v: bfloat16 [4096, 32, 128], P('ctx', 'head'), may hold values from -16 to 16
- lin_decay: float32 [32, 4096], P('head', 'ctx'), may hold values from -1.5 to 0
- norm_gain: float32 [32, 128], P('head'), may hold values from 0.1 to 1.9
- soft_q: bfloat16 [4096, 32, 128], P('ctx', 'head'), may hold values from -5 to 5
- soft_k: bfloat16 [4096, 32, 128], P('ctx', 'head'), may hold values from -5 to 5
- soft_v: bfloat16 [4096, 32, 128], P('ctx', 'head'), may hold values from -5 to 5
- out_grad: bfloat16 [4096, 32, 128], P('ctx', 'head'), may hold values from -5 to 5
- block_lists: int32 [32, 16], P('ctx'), may hold values from 0 to 30, as said below
- block_counts: int32 [32], P('ctx'), may hold values from 0 to 16, as said below
Outputs:
- lin_dq: bfloat16 [4096, 32, 128], P('ctx', 'head')
- lin_dk: bfloat16 [4096, 32, 128], P('ctx', 'head')
- lin_dv: bfloat16 [4096, 32, 128], P('ctx', 'head')
- soft_dq: bfloat16 [4096, 32, 128], P('ctx', 'head')
- soft_dk: bfloat16 [4096, 32, 128], P('ctx', 'head')
- soft_dv: bfloat16 [4096, 32, 128], P('ctx', 'head')
Inputs may be any that keep to these rules, and one draw needn't show every extreme that they name: `block_lists`: entries past block_counts[b] are 0. The first block_counts[b] entries of query block b are distinct blocks that lie before the span of 128 tokens holding b. All query blocks of one span name together at most one block of each other span. In every span after the first, some query block names every block that its span names; from the second span on these include block 0, and from the third on also the last block before the span. `block_counts`: in span i of 128 tokens some query block has the count min(i, 16); every count is at most that; counts are 0 only in the first span.
All inputs are finite; a program needn't handle non-finite values.
Results may differ from a plain program's by a relative error of at most 0.011.
Values may be sent and summed in bfloat16 or wider, within the bound.
A program may use at most 128 MiB of HBM per device.

v0:
```python
import jax
import jax.numpy as jnp
from jax import lax
from jax.sharding import PartitionSpec as P

BLK = 128
NSEL = 16
epsilon = 1e-05
exact_precision = lax.Precision.HIGHEST


def carried_in(part, axis, combine, identity, reverse):
    count = lax.axis_size(axis)
    place = lax.axis_index(axis)
    ahead = count - 1 - place if reverse else place
    gathered = jax.tree.map(lambda a: lax.all_gather(a, axis), part)
    state = jax.tree.map(lambda a, e: jnp.zeros_like(a) + jnp.asarray(e, a.dtype), part, identity)

    def one(lap, state):
        source = count - 1 - lap if reverse else lap
        return combine(
            state, jax.tree.map(lambda a: lax.dynamic_index_in_dim(a, source, 0, False), gathered)
        )

    return lax.fori_loop(0, ahead, one, state)


def decay_tables(decays):
    running = jnp.cumsum(decays, axis=1)
    finish = running[:, -1]
    length = decays.shape[1]
    below_diag = (jnp.arange(length)[:, None] >= jnp.arange(length)[None, :])[None]
    spread = running[:, :, None] - running[:, None, :]
    within = jnp.where(below_diag, jnp.exp(jnp.where(below_diag, spread, 0.0)), 0.0)
    return (jnp.exp(finish), jnp.exp(finish[:, None] - running), jnp.exp(running), within)


def chain_join(earlier, later):
    return (earlier[0] * later[0], later[0][:, None, None] * earlier[1] + later[1])


def sparse_grads(queries, grads_out, key_rows, value_rows, allowed):
    score_scale = queries.shape[-1] ** (-0.5)
    scores = (
        jnp.einsum("bqhd,bkhd->bhqk", queries, key_rows, preferred_element_type=jnp.float32)
        * score_scale
    )
    key_mask = allowed[:, None]
    scores = jnp.where(key_mask, scores, -1e30)
    row_max = jnp.max(scores, axis=-1, keepdims=True)
    weights = jnp.where(key_mask, jnp.exp(scores - row_max), 0.0)
    softmax_probs = weights / jnp.sum(weights, axis=-1, keepdims=True)
    rounded = softmax_probs.astype(jnp.bfloat16)
    outputs = jnp.einsum("bhqk,bkhd->bqhd", rounded, value_rows, preferred_element_type=jnp.float32)
    row_delta = jnp.sum(grads_out.astype(jnp.float32) * outputs, axis=-1)
    grad_probs = jnp.einsum(
        "bqhd,bkhd->bhqk", grads_out, value_rows, preferred_element_type=jnp.float32
    )
    grad_scores = (
        softmax_probs * (grad_probs - jnp.transpose(row_delta, (0, 2, 1))[..., None])
    ).astype(jnp.bfloat16)
    query_gradient = (
        jnp.einsum("bhqk,bkhd->bqhd", grad_scores, key_rows, preferred_element_type=jnp.float32)
        * score_scale
    )
    key_gradient = (
        jnp.einsum("bhqk,bqhd->bkhd", grad_scores, queries, preferred_element_type=jnp.float32)
        * score_scale
    )
    value_gradient = jnp.einsum(
        "bhqk,bqhd->bkhd", rounded, grads_out, preferred_element_type=jnp.float32
    )
    return (query_gradient, key_gradient, value_gradient)


def local(
    lin_q,
    lin_k,
    lin_v,
    lin_decay,
    norm_gain,
    soft_q,
    soft_k,
    soft_v,
    out_grad,
    block_lists,
    block_counts,
):
    tok_rows, heads_here, head_width = lin_q.shape
    blocks_here = tok_rows // BLK
    span_count = lax.axis_size("ctx")
    own_span = lax.axis_index("ctx")
    total_width = heads_here * lax.axis_size("head") * head_width
    complete_query = lin_q.astype(jnp.float32)
    complete_key = lin_k.astype(jnp.float32)
    complete_value = lin_v.astype(jnp.float32)
    carry_decay, trailing_decay, leading_decay, within = decay_tables(lin_decay)
    state_here = jnp.einsum(
        "boz,bor->ozr",
        complete_key * trailing_decay.T[:, :, None],
        complete_value,
        precision=exact_precision,
    )
    identity = (jnp.ones_like(carry_decay), jnp.zeros_like(state_here))
    incoming_state = carried_in((carry_decay, state_here), "ctx", chain_join, identity, False)[1]
    pair_weights = (
        jnp.einsum("thk,shk->hts", lin_q, lin_k, preferred_element_type=jnp.float32) * within
    )
    layer_out = jnp.einsum("hts,shv->thv", pair_weights, complete_value, precision=exact_precision)
    layer_out = layer_out + leading_decay.T[:, :, None] * jnp.einsum(
        "wfg,fgl->wfl", complete_query, incoming_state, precision=exact_precision
    )
    squares = lax.psum(jnp.sum(layer_out * layer_out, axis=(1, 2)), "head")
    root_mean = jnp.sqrt(squares / total_width + epsilon)
    norm_scale = norm_gain[None]
    all_lists, all_counts = (
        lax.all_gather(block_lists, "ctx", axis=0, tiled=True),
        lax.all_gather(block_counts, "ctx", axis=0, tiled=True),
    )
    entries = blocks_here * NSEL
    every_live = (
        jnp.arange(NSEL)[None, None, :] < all_counts.reshape(span_count, blocks_here)[:, :, None]
    ).reshape(span_count, entries)
    owner_hits = every_live & (all_lists // blocks_here == own_span)
    wanted_here = jnp.max(jnp.where(owner_hits, all_lists % blocks_here, -1), axis=1)
    my_live = jnp.arange(NSEL)[None, :] < block_counts[:, None]
    flat_owner = (block_lists // blocks_here).reshape(entries)
    flat_live = my_live.reshape(entries)
    key_blocks = soft_k.reshape(blocks_here, BLK, heads_here, head_width)
    value_blocks = soft_v.reshape(blocks_here, BLK, heads_here, head_width)
    owners = jnp.arange(span_count)
    matches = flat_live[None, :] & (flat_owner[None, :] == owners[:, None])
    wanted_ids = jnp.max(jnp.where(matches, block_lists.reshape(entries)[None, :], -1), axis=1)
    empty_slot = jnp.zeros((span_count, BLK, heads_here, head_width), jnp.bfloat16)
    shard_piece = (
        lax.all_gather(soft_k, "ctx", axis=0, tiled=True),
        lax.all_gather(soft_v, "ctx", axis=0, tiled=True),
    )
    row_count = shard_piece[0].shape[0]
    token_index = wanted_ids[:, None] * BLK + jnp.arange(BLK)[None, :]
    usable = ((wanted_ids[:, None] >= 0) & (token_index >= 0) & (token_index < row_count))[
        :, :, None, None
    ]
    safe_index = jnp.clip(token_index, 0, row_count - 1)
    new_keys = jnp.where(usable, shard_piece[0][safe_index], empty_slot)
    new_values = jnp.where(usable, shard_piece[1][safe_index], empty_slot)
    listed_keys = jnp.take(new_keys, flat_owner, axis=0).reshape(
        blocks_here, NSEL * BLK, heads_here, head_width
    )
    listed_values = jnp.take(new_values, flat_owner, axis=0).reshape(
        blocks_here, NSEL * BLK, heads_here, head_width
    )
    key_rows = jnp.concatenate([key_blocks, listed_keys], axis=1)
    value_rows = jnp.concatenate([value_blocks, listed_values], axis=1)
    causal = jnp.arange(BLK)[:, None] >= jnp.arange(BLK)[None, :]
    remote_mask = jnp.broadcast_to(
        jnp.repeat(my_live, BLK, axis=1)[:, None, :], (blocks_here, BLK, NSEL * BLK)
    )
    allowed = jnp.concatenate(
        [jnp.broadcast_to(causal, (blocks_here, BLK, BLK)), remote_mask], axis=2
    )
    query_blocks = soft_q.reshape(blocks_here, BLK, heads_here, head_width)
    grad_blocks = out_grad.reshape(blocks_here, BLK, heads_here, head_width)
    query_gradient, key_gradient, value_gradient = sparse_grads(
        query_blocks, grad_blocks, key_rows, value_rows, allowed
    )
    soft_dq = query_gradient.reshape(tok_rows, heads_here, head_width).astype(jnp.bfloat16)
    routing = (
        flat_live[None, :] & (flat_owner[None, :] == jnp.arange(span_count)[:, None])
    ).astype(jnp.float32)
    remote_key = key_gradient[:, BLK:].reshape(entries, BLK, heads_here, head_width)
    remote_value = value_gradient[:, BLK:].reshape(entries, BLK, heads_here, head_width)
    part_key = jnp.einsum("oe,exhd->oxhd", routing, remote_key, precision=exact_precision).astype(
        jnp.bfloat16
    )
    part_value = jnp.einsum(
        "oe,exhd->oxhd", routing, remote_value, precision=exact_precision
    ).astype(jnp.bfloat16)
    back_key, back_value = (
        lax.all_to_all(part_key, "ctx", split_axis=0, concat_axis=0, tiled=True),
        lax.all_to_all(part_value, "ctx", split_axis=0, concat_axis=0, tiled=True),
    )
    placing = (wanted_here[:, None] == jnp.arange(blocks_here)[None, :]).astype(jnp.float32)
    added_key = jnp.einsum(
        "rb,rxhd->bxhd", placing, back_key.astype(jnp.float32), precision=exact_precision
    ).reshape(tok_rows, heads_here, head_width)
    added_value = jnp.einsum(
        "rb,rxhd->bxhd", placing, back_value.astype(jnp.float32), precision=exact_precision
    ).reshape(tok_rows, heads_here, head_width)
    soft_dk = (key_gradient[:, :BLK].reshape(tok_rows, heads_here, head_width) + added_key).astype(
        jnp.bfloat16
    )
    value_total = value_gradient[:, :BLK].reshape(tok_rows, heads_here, head_width) + added_value
    soft_dv = value_total.astype(jnp.bfloat16)
    cotangent = out_grad.astype(jnp.float32) + value_total
    inner_total = lax.psum(jnp.sum(norm_scale * cotangent * layer_out, axis=(1, 2)), "head")
    linear_cotangent = (
        norm_scale * cotangent / root_mean[:, None, None]
        - layer_out * (inner_total / (total_width * root_mean**3))[:, None, None]
    )
    reverse_state = carried_in(
        (
            carry_decay,
            jnp.einsum(
                "boz,bor->ozr",
                complete_query * leading_decay.T[:, :, None],
                linear_cotangent,
                precision=exact_precision,
            ),
        ),
        "ctx",
        chain_join,
        identity,
        True,
    )[1]
    grad_pair = (
        jnp.einsum("thv,shv->hts", linear_cotangent, complete_value, precision=exact_precision)
        * within
    )
    lin_dq = jnp.einsum("hts,shk->thk", grad_pair, complete_key, precision=exact_precision)
    lin_dq = lin_dq + leading_decay.T[:, :, None] * jnp.einsum(
        "fqs,qrs->fqr", linear_cotangent, incoming_state, precision=exact_precision
    )
    lin_dk = jnp.einsum("hts,thk->shk", grad_pair, complete_query, precision=exact_precision)
    lin_dk = lin_dk + trailing_decay.T[:, :, None] * jnp.einsum(
        "fut,ujt->fuj", complete_value, reverse_state, precision=exact_precision
    )
    lin_dv = jnp.einsum("hts,thv->shv", pair_weights, linear_cotangent, precision=exact_precision)
    lin_dv = lin_dv + trailing_decay.T[:, :, None] * jnp.einsum(
        "zpu,pux->zpx", complete_key, reverse_state, precision=exact_precision
    )
    return (
        lin_dq.astype(jnp.bfloat16),
        lin_dk.astype(jnp.bfloat16),
        lin_dv.astype(jnp.bfloat16),
        soft_dq,
        soft_dk,
        soft_dv,
    )


def solution(mesh):
    in_specs = (
        P("ctx", "head", None),
        P("ctx", "head", None),
        P("ctx", "head", None),
        P("head", "ctx"),
        P("head", None),
        P("ctx", "head", None),
        P("ctx", "head", None),
        P("ctx", "head", None),
        P("ctx", "head", None),
        P("ctx", None),
        P("ctx"),
    )
    out_specs = (
        P("ctx", "head", None),
        P("ctx", "head", None),
        P("ctx", "head", None),
        P("ctx", "head", None),
        P("ctx", "head", None),
        P("ctx", "head", None),
    )
    return jax.shard_map(local, mesh=mesh, in_specs=in_specs, out_specs=out_specs, check_vma=False)
```

profile of v0, /device:TPU:32, one launch (start us, length us, event | category | flops | bytes accessed | tf_op | source)
XLA Modules:
  0.0 770.6 jit_solution(8444766852220716513)
XLA Ops:
  11.1 2.1 fusion.51
  17.2 1.3 add_bitcast_fusion
  18.5 76.2 %all-gather.11.cloned.1.call-done = bf16[4096,4,128]{2,1,0:T(4,128)(2,1)} async-done(((bf16[128,4,128]{2,1,0:T(4,128)(2,1)}), bf16[4096,4,128]{2,1,0:T(4,128)(2,1)}) %all-gather.11.cloned.1.call-update) | async-done | bytes 4194320 | tf_op jit(solution)/shard_map/all_gather | solution.py:137
  94.7 30.5 %gather_fusion.1 = bf16[4096,4,128]{2,1,0:T(4,128)(2,1)} fusion(bf16[4096,4,128]{2,1,0:T(4,128)(2,1)} %all-gather.11.cloned.1.call-done, s32[4096]{0:T(1024)S(1)} %fusion.73), kind=kCustom, calls=%fused_computation.3 | custom fusion | bytes 8404992 | tf_op jit(solution)/shard_map/gather | solution.py:146
  125.2 50.7 %all-gather.9.cloned.1.call-done = bf16[4096,4,128]{2,1,0:T(4,128)(2,1)} async-done(((bf16[128,4,128]{2,1,0:T(4,128)(2,1)}), bf16[4096,4,128]{2,1,0:T(4,128)(2,1)}) %all-gather.9.cloned.1.call-update) | async-done | bytes 4194320 | tf_op jit(solution)/shard_map/all_gather | solution.py:136
  175.9 30.5 %gather_fusion = bf16[4096,4,128]{2,1,0:T(4,128)(2,1)} fusion(bf16[4096,4,128]{2,1,0:T(4,128)(2,1)} %all-gather.9.cloned.1.call-done, s32[4096]{0:T(1024)S(1)} %fusion.73), kind=kCustom, calls=%fused_computation.2 | custom fusion | bytes 8404992 | tf_op jit(solution)/shard_map/gather | solution.py:145
  206.4 6.7 copy_select_fusion
  213.0 3.2 gather_fusion.3
  216.2 4.4 gather_fusion.2
  220.6 3.4 broadcast_select_fusion
  224.2 3.9 fusion.102
  228.1 2.7 fusion.24
  231.8 1.7 copy-done.1
  233.5 7.4 fusion.18
  241.0 4.2 copy.213
  245.2 6.6 all-to-all-start
  253.3 170.3 %all-reduce.1 = f32[128]{0:T(128)S(1)} all-reduce(f32[128]{0:T(128)S(1)} %dynamic-update-slice.1), channel_id=2, replica_groups=mesh['ctx'=32,'head'=8] {'ctx'}, use_global_device_ids=true, to_apply=%add.1 | all-reduce | flops 128 | bytes 1024
  423.8 37.6 %all-gather.3 = s32[32,1,16]{2,1,0:T(1,128)S(1)} all-gather(s32[1,1,16]{2,1,0:T(1,128)S(1)} %bitcast.233), channel_id=1, replica_groups=mesh['ctx'=32,'head'=8] {'ctx'}, dimensions={0}, use_global_device_ids=true | all-gather | bytes 2112 | tf_op jit(solution)/shard_map/all_gather | solution.py:117
  462.2 18.1 %all-reduce = s32[32]{0:T(128)S(1)} all-reduce(s32[32]{0:T(128)S(1)} %dynamic-update-slice), channel_id=1, replica_groups=mesh['ctx'=32,'head'=8] {'ctx'}, use_global_device_ids=true, to_apply=%add | all-reduce | flops 32 | bytes 256
  482.1 1.1 while.26
  482.1 1.1 bitcast_add_fusion.4
  483.8 4.6 fusion.12
  488.4 2.0 multiply_reduce_fusion.1
  490.5 12.6 %all-reduce.2 = (f32[128]{0:T(128)S(1)}, f32[128]{0:T(128)S(1)}) all-reduce(f32[128]{0:T(128)S(1)} %get-tuple-element.168, f32[128]{0:T(128)S(1)} %get-tuple-element.167), channel_id=1, replica_groups=mesh['ctx'=32,'head'=8] {'head'}, use_global_device_ids=true, to_apply=%region_10.12 | all-reduce | flops 256 | bytes 2048 | tf_op jit(solution)/shard_map/psum | solution.py:196
  503.1 1.2 multiply_subtract_fusion
  504.4 2.1 fusion.48
  507.4 1.8 copy.241
  509.2 1.9 fusion.43
  511.1 3.1 fusion.9
  515.2 1.8 copy-done.2
  517.0 7.2 fusion.21
  524.3 4.1 copy.250
  528.4 38.5 %all-to-all-start.1 = ((bf16[32,128,4,128]{3,2,1,0:T(4,128)(2,1)}), bf16[32,128,4,128]{3,2,1,0:T(4,128)(2,1)}, u32[]{:S(2)}, u32[]{:S(2)}) async-start(bf16[32,128,4,128]{3,2,1,0:T(4,128)(2,1)} %copy.250), calls=%async_computation.1 | async-start | bytes 8388608 | tf_op jit(solution)/shard_map/all_to_all | solution.py:180
  566.9 2.5 fusion.42
  570.2 128.2 %all-to-all-done.1 = bf16[32,128,4,128]{3,2,1,0:T(4,128)(2,1)} async-done(((bf16[32,128,4,128]{3,2,1,0:T(4,128)(2,1)}), bf16[32,128,4,128]{3,2,1,0:T(4,128)(2,1)}, u32[]{:S(2)}, u32[]{:S(2)}) %all-to-all-start.1) | async-done | bytes 4194336 | tf_op jit(solution)/shard_map/all_to_all | solution.py:180
  698.3 4.6 fusion.10
  708.6 53.2 %while.27 = (s32[]{:T(128)}, f32[4,128,128]{2,1,0:T(8,128)S(1)}, s32[]{:T(128)}, f32[32,4]{1,0:T(8,128)}, f32[32,4,128,128]{3,2,1,0:T(8,128)}, /*index=5*/s32[]{:T(128)}, s32[]{:T(128)}, s32[]{:T(128)}, s32[]{:T(128)}) while((s32[]{:T(128)}, f32[4,128,128]{2,1,0:T(8,128)S(1)}, s32[]{:T(128)}, f32[32,4]{1,0:T(8,128)}, ...), condition=%wide.region_12.14_spmd, body=%wide.region_11.13_spmd.sunk | while | flops 131078 | bytes 786635 | solution.py:25
  709.3 1.1 bitcast_add_fusion.5
  711.1 1.1 bitcast_add_fusion.5
  712.9 1.1 bitcast_add_fusion.5
  714.6 1.1 bitcast_add_fusion.5
  716.4 1.1 bitcast_add_fusion.5
  718.2 1.1 bitcast_add_fusion.5
  720.0 1.1 bitcast_add_fusion.5
  721.7 1.1 bitcast_add_fusion.5
  723.5 1.1 bitcast_add_fusion.5
  727.1 1.1 bitcast_add_fusion.5
  728.8 1.1 bitcast_add_fusion.5
  (165 shorter events, 63.9 us)
Async XLA Ops:
  7.2 217.0 %copy-start = (bf16[128,4,128]{2,1,0:T(4,128)(2,1)S(1)}, bf16[128,4,128]{2,1,0:T(4,128)(2,1)}, u32[]{:S(2)}) copy-start(bf16[128,4,128]{2,1,0:T(4,128)(2,1)} %param.22) | copy-start | bytes 393220
  7.2 87.5 %all-gather.11.cloned.1.call-start = ((), (), s32[]{:S(2)}) async-start(), calls=%async_computation.3 | async-start | bytes 4325376 | tf_op jit(solution)/shard_map/all_gather | solution.py:137
  7.9 168.0 %all-gather.9.cloned.1.call-start = ((), (), s32[]{:S(2)}) async-start(), calls=%async_computation.2 | async-start | bytes 4325376 | tf_op jit(solution)/shard_map/all_gather | solution.py:136
  8.7 473.4 %all-gather.13.cloned.1.call-start = ((), (), s32[]{:S(2)}) async-start(), calls=%async_computation.4 | async-start | bytes 8650752 | tf_op jit(solution)/shard_map/all_gather | solution.py:16
  9.7 471.1 %copy-start.15 = (f32[4,128]{1,0:T(4,128)}, f32[4,128]{1,0:T(4,128)S(1)}, u32[]{:S(2)}) copy-start(f32[4,128]{1,0:T(4,128)S(1)} %reduce_window_sum.11) | copy-start | bytes 6148
  10.5 0.6 copy-start.17
  14.2 210.0 %copy-start.13 = (bf16[128,4,128]{2,0,1:T(8,128)(2,1)}, bf16[128,4,128]{2,0,1:T(8,128)(2,1)S(1)}, u32[]{:S(2)}) copy-start(bf16[128,4,128]{2,0,1:T(8,128)(2,1)S(1)} %copy.353) | copy-start | bytes 393220
  14.8 218.7 %copy-start.23 = (pred[16]{0:T(512)(128)(4,1)}, pred[16]{0:T(512)(128)(4,1)S(1)}, u32[]{:S(2)}) copy-start(pred[16]{0:T(512)(128)(4,1)S(1)} %iota_compare_fusion.4) | copy-start | bytes 52
  224.2 3.9 copy-start.3
  228.1 3.4 copy-start.25
  228.1 2.7 copy-start.7
  231.5 2.0 copy-start.1
  231.5 2.0 copy-start.21
  245.1 6.7 copy-start.27
  245.1 235.7 %copy-start.5 = (bf16[128,4,128]{2,1,0:T(4,128)(2,1)S(1)}, bf16[128,4,128]{2,1,0:T(4,128)(2,1)}, u32[]{:S(2)}) copy-start(bf16[128,4,128]{2,1,0:T(4,128)(2,1)} %param.17) | copy-start | bytes 393220
  245.2 235.7 %copy-start.6 = (bf16[128,4,128]{2,1,0:T(4,128)(2,1)S(1)}, bf16[128,4,128]{2,1,0:T(4,128)(2,1)}, u32[]{:S(2)}) copy-start(bf16[128,4,128]{2,1,0:T(4,128)(2,1)} %param.18) | copy-start | bytes 393220
  245.2 235.9 %copy-start.4 = (bf16[128,4,128]{2,1,0:T(4,128)(2,1)S(1)}, bf16[128,4,128]{2,1,0:T(4,128)(2,1)}, u32[]{:S(2)}) copy-start(bf16[128,4,128]{2,1,0:T(4,128)(2,1)} %param.19) | copy-start | bytes 393220
  245.2 238.6 %all-to-all-start = ((bf16[32,128,4,128]{3,2,1,0:T(4,128)(2,1)}), bf16[32,128,4,128]{3,2,1,0:T(4,128)(2,1)}, u32[]{:S(2)}, u32[]{:S(2)}) async-start(bf16[32,128,4,128]{3,2,1,0:T(4,128)(2,1)} %copy.213), calls=%async_computation | async-start | bytes 8388608 | tf_op jit(solution)/shard_map/all_to_all | solution.py:181
  251.8 456.8 %all-gather.15.cloned.1.call-start = ((), (), s32[]{:S(2)}) async-start(), calls=%async_computation.5 | async-start | bytes 8650752 | tf_op jit(solution)/shard_map/all_gather | solution.py:16
  481.1 2.1 copy-start.9
  483.2 0.6 copy-start.20
  483.8 4.7 copy-start.11
  509.2 1.9 copy-start.8
  509.2 1.9 copy-start.26
  514.9 2.1 copy-start.2
  514.9 2.1 copy-start.22
  514.9 2.1 copy-start.24
  528.4 38.5 %copy-start.14 = (bf16[128,4,128]{2,0,1:T(8,128)(2,1)S(1)}, bf16[128,4,128]{2,0,1:T(8,128)(2,1)}, u32[]{:S(2)}) copy-start(bf16[128,4,128]{2,0,1:T(8,128)(2,1)} %copy-done.13) | copy-start | bytes 393220
  528.4 170.0 %all-to-all-start.1 = ((bf16[32,128,4,128]{3,2,1,0:T(4,128)(2,1)}), bf16[32,128,4,128]{3,2,1,0:T(4,128)(2,1)}, u32[]{:S(2)}, u32[]{:S(2)}) async-start(bf16[32,128,4,128]{3,2,1,0:T(4,128)(2,1)} %copy.250), calls=%async_computation.1 | async-start | bytes 8388608 | tf_op jit(solution)/shard_map/all_to_all | solution.py:180
  569.4 135.3 %copy-start.12 = (bf16[128,4,128]{2,0,1:T(8,128)(2,1)S(1)}, bf16[128,4,128]{2,0,1:T(8,128)(2,1)}, u32[]{:S(2)}) copy-start(bf16[128,4,128]{2,0,1:T(8,128)(2,1)} %get-tuple-element.193) | copy-start | bytes 393220
  569.4 136.1 %copy-start.16 = (f32[4,128]{1,0:T(4,128)S(1)}, f32[4,128]{1,0:T(4,128)}, u32[]{:S(2)}) copy-start(f32[4,128]{1,0:T(4,128)} %copy-done.15) | copy-start | bytes 6148
  569.4 136.7 %copy-start.19 = (f32[128,4]{0,1:T(4,128)S(1)}, f32[128,4]{0,1:T(4,128)}, u32[]{:S(2)}) copy-start(f32[128,4]{0,1:T(4,128)} %get-tuple-element.196) | copy-start | bytes 6148
  570.2 137.8 %copy-start.10 = (f32[4,128,128]{2,1,0:T(8,128)S(1)}, f32[4,128,128]{2,1,0:T(8,128)}, u32[]{:S(2)}) copy-start(f32[4,128,128]{2,1,0:T(8,128)} %copy-done.9) | copy-start | bytes 786436
  705.5 56.4 %copy-start.18 = (f32[128,4]{0,1:T(4,128)S(1)}, f32[128,4]{0,1:T(4,128)}, u32[]{:S(2)}) copy-start(f32[128,4]{0,1:T(4,128)} %copy-done.17) | copy-start | bytes 6148
Sparse Core Ops, SparseCore 0:
  10.6 84.0 all-gather.10
  97.3 78.5 all-gather.8
  178.5 149.4 all-gather.12
  506.6 193.3 all-gather.14
where the time goes:
time: 773 us; the launch traced here: 771 us
  waiting for transfers between devices  256 us (33%)
  blocking collectives  239 us (31%)
  local copies, waits for them, and re-layouts  114 us (15%)
  other arithmetic  53.3 us (7%)
  matrix products  47 us (6%)
  starting transfers between devices  45.2 us (6%)
  between operations  15.6 us (2%)
    unnamed x2, blocking collectives  188 us
    all_to_all x1, waiting for transfers between devices, local(): lax.all_to_all(part_key, 'ctx', split_axis=0, concat_axis=0, tiled=True)  128 us
    all_gather x1, waiting for transfers between devices, local(): lax.all_gather(soft_v, 'ctx', axis=0, tiled=True)  76.2 us
    all_gather x1, waiting for transfers between devices, local(): lax.all_gather(soft_k, 'ctx', axis=0, tiled=True)  50.7 us
    all_to_all x1, starting transfers between devices, local(): lax.all_to_all(part_key, 'ctx', split_axis=0, concat_axis=0, tiled=True)  38.5 us
    all_gather x1, blocking collectives, local(): lax.all_gather(block_lists, 'ctx', axis=0, tiled=True)  37.6 us
    add x31, other arithmetic, chain_join(): later[0][:, None, None] * earlier[1] + later[1]  32.7 us
    gather x1, local copies, waits for them, and re-layouts, local(): new_keys = jnp.where(usable, shard_piece[0][safe_index], empty_slot)  30.5 us
  transfers between devices with their start and end apart: 6, of which 3 were waited for; matrix products, arithmetic and copies ran while one was open for 19% of the time, Pallas kernels for 0%

commit v1 on v0

--- a/solution.py
+++ b/solution.py
@@ -114,7 +114,9 @@
     root_mean = jnp.sqrt(squares / total_width + epsilon)
     norm_scale = norm_gain[None]
     all_lists, all_counts = (
-        lax.all_gather(block_lists, "ctx", axis=0, tiled=True),
+        jnp.concatenate(
+            lax.all_to_all(jnp.stack([block_lists] * lax.axis_size("ctx")), "ctx", 0, 0), axis=0
+        ),
         lax.all_gather(block_counts, "ctx", axis=0, tiled=True),
     )
     entries = blocks_here * NSEL

time: 773 us -> 747 us (0.966); the launches traced: 771 us -> 736 us
  blocking collectives: 239 us -> 200 us
  starting transfers between devices: 45.2 us -> 59.1 us
  waiting for transfers between devices: 256 us -> 245 us
    all_gather x1 -> x0, blocking collectives: 37.6 us -> none  [local(): lax.all_gather(block_lists, 'ctx', axis=0, tiled=True)]
    all_gather x1, waiting for transfers between devices: 76.2 us -> 63.7 us  [local(): lax.all_gather(soft_v, 'ctx', axis=0, tiled=True)]
    all_to_all x0 -> x1, starting transfers between devices: none -> 11.4 us  [local(): lax.all_to_all(jnp.stack([block_lists] * lax.axis_size('ctx')), 'ctx', 0, 0)]
  transfers between devices with their start and end apart: 6 -> 7, of which waited for: 3 -> 3; matrix products, arithmetic and copies ran while one was open for 19% -> 20% of each run, Pallas kernels for 0% -> 0%
where the time goes in v1:
time: 747 us; the launch traced here: 736 us
  waiting for transfers between devices  245 us (33%)
  blocking collectives  200 us (27%)
  local copies, waits for them, and re-layouts  115 us (15%)
  starting transfers between devices  59.1 us (8%)
  other arithmetic  53.4 us (7%)
  matrix products  47.1 us (6%)
  between operations  15.8 us (2%)
    unnamed x2, blocking collectives  187 us
    all_to_all x1, waiting for transfers between devices, local(): lax.all_to_all(part_key, 'ctx', split_axis=0, concat_axis=0, tiled=True)  129 us
    all_gather x1, waiting for transfers between devices, local(): lax.all_gather(soft_v, 'ctx', axis=0, tiled=True)  63.7 us
    all_gather x1, waiting for transfers between devices, local(): lax.all_gather(soft_k, 'ctx', axis=0, tiled=True)  50.6 us
    all_to_all x1, starting transfers between devices, local(): lax.all_to_all(part_key, 'ctx', split_axis=0, concat_axis=0, tiled=True)  40.9 us
    add x31, other arithmetic, chain_join(): later[0][:, None, None] * earlier[1] + later[1]  32.7 us
    gather x1, local copies, waits for them, and re-layouts, local(): new_values = jnp.where(usable, shard_piece[1][safe_index], empty_slot)  30.5 us
    gather x1, local copies, waits for them, and re-layouts, local(): new_keys = jnp.where(usable, shard_piece[0][safe_index], empty_slot)  30.5 us
  transfers between devices with their start and end apart: 7, of which 3 were waited for; matrix products, arithmetic and copies ran while one was open for 20% of the time, Pallas kernels for 0%

profile of v1, /device:TPU:32, one launch (start us, length us, event | category | flops | bytes accessed | tf_op | source)
XLA Modules:
  0.0 735.8 jit_solution(5333332545220023563)
XLA Ops:
  11.0 2.2 fusion.51
  13.2 1.3 stack.2
  14.5 11.4 %all-to-all-start = ((s32[32,1,16]{2,1,0:T(1,128)}), s32[32,1,16]{2,1,0:T(1,128)S(1)}, u32[]{:S(2)}, u32[]{:S(2)}) async-start(s32[32,1,16]{2,1,0:T(1,128)} %stack.2), calls=%async_computation | async-start | bytes 32768 | tf_op jit(solution)/shard_map/all_to_all | solution.py:118
  29.8 1.3 add_bitcast_fusion
  31.1 63.7 %all-gather.10.cloned.1.call-done = bf16[4096,4,128]{2,1,0:T(4,128)(2,1)} async-done(((bf16[128,4,128]{2,1,0:T(4,128)(2,1)}), bf16[4096,4,128]{2,1,0:T(4,128)(2,1)}) %all-gather.10.cloned.1.call-update) | async-done | bytes 4194320 | tf_op jit(solution)/shard_map/all_gather | solution.py:139
  94.8 30.5 %gather_fusion.1 = bf16[4096,4,128]{2,1,0:T(4,128)(2,1)} fusion(bf16[4096,4,128]{2,1,0:T(4,128)(2,1)} %all-gather.10.cloned.1.call-done, s32[4096]{0:T(1024)S(1)} %fusion.73), kind=kCustom, calls=%fused_computation.3 | custom fusion | bytes 8404992 | tf_op jit(solution)/shard_map/gather | solution.py:148
  125.4 50.6 %all-gather.8.cloned.1.call-done = bf16[4096,4,128]{2,1,0:T(4,128)(2,1)} async-done(((bf16[128,4,128]{2,1,0:T(4,128)(2,1)}), bf16[4096,4,128]{2,1,0:T(4,128)(2,1)}) %all-gather.8.cloned.1.call-update) | async-done | bytes 4194320 | tf_op jit(solution)/shard_map/all_gather | solution.py:138
  176.0 30.5 %gather_fusion = bf16[4096,4,128]{2,1,0:T(4,128)(2,1)} fusion(bf16[4096,4,128]{2,1,0:T(4,128)(2,1)} %all-gather.8.cloned.1.call-done, s32[4096]{0:T(1024)S(1)} %fusion.73), kind=kCustom, calls=%fused_computation.2 | custom fusion | bytes 8404992 | tf_op jit(solution)/shard_map/gather | solution.py:147
  206.5 6.7 copy_select_fusion
  213.2 3.2 gather_fusion.3
  216.3 4.4 gather_fusion.2
  220.7 3.4 broadcast_select_fusion
  224.3 3.9 fusion.102
  228.2 2.7 fusion.24
  231.9 1.7 copy-done.1
  233.7 7.5 %fusion.18 = bf16[32,128,4,128]{3,0,2,1:T(8,128)(2,1)S(1)} fusion(f32[16,128,4,128]{3,1,0,2:T(8,128)S(1)} %bitcast.219, s32[16]{0:T(128)S(1)} %bitcast.232, pred[16]{0:T(512)(128)(4,1)S(1)} %iota_compare_fusion.4), kind=kOutput, calls=%fused_computation.32 | convolution fusion | flops 404751360 | bytes 8388688 | tf_op jit(solution)/shard_map/oe,exhd->oxhd/dot_general | solution.py:178
  241.2 4.2 copy.264
  245.4 6.6 all-to-all-start.1
  253.6 170.3 %all-reduce.1 = f32[128]{0:T(128)S(1)} all-reduce(f32[128]{0:T(128)S(1)} %dynamic-update-slice.1), channel_id=2, replica_groups=mesh['ctx'=32,'head'=8] {'ctx'}, use_global_device_ids=true, to_apply=%add.1 | all-reduce | flops 128 | bytes 1024
  424.7 17.2 %all-reduce = s32[32]{0:T(128)S(1)} all-reduce(s32[32]{0:T(128)S(1)} %dynamic-update-slice), channel_id=1, replica_groups=mesh['ctx'=32,'head'=8] {'ctx'}, use_global_device_ids=true, to_apply=%add | all-reduce | flops 32 | bytes 256
  443.8 1.1 while.26
  443.8 1.1 bitcast_add_fusion.4
  445.5 4.6 fusion.12
  450.2 2.0 multiply_reduce_fusion.1
  452.2 12.9 %all-reduce.2 = (f32[128]{0:T(128)S(1)}, f32[128]{0:T(128)S(1)}) all-reduce(f32[128]{0:T(128)S(1)} %get-tuple-element.174, f32[128]{0:T(128)S(1)} %get-tuple-element.173), channel_id=1, replica_groups=mesh['ctx'=32,'head'=8] {'head'}, use_global_device_ids=true, to_apply=%region_10.12 | all-reduce | flops 256 | bytes 2048 | tf_op jit(solution)/shard_map/psum | solution.py:198
  465.1 1.2 multiply_subtract_fusion
  466.3 2.1 fusion.48
  469.3 1.8 copy.292
  471.2 1.9 fusion.43
  473.1 3.1 fusion.9
  477.2 1.8 copy-done.2
  479.0 7.2 fusion.21
  486.2 4.1 copy.301
  490.3 40.9 %all-to-all-start.2 = ((bf16[32,128,4,128]{3,2,1,0:T(4,128)(2,1)}), bf16[32,128,4,128]{3,2,1,0:T(4,128)(2,1)}, u32[]{:S(2)}, u32[]{:S(2)}) async-start(bf16[32,128,4,128]{3,2,1,0:T(4,128)(2,1)} %copy.301), calls=%async_computation.2 | async-start | bytes 8388608 | tf_op jit(solution)/shard_map/all_to_all | solution.py:182
  531.3 2.4 fusion.42
  534.6 128.8 %all-to-all-done.2 = bf16[32,128,4,128]{3,2,1,0:T(4,128)(2,1)} async-done(((bf16[32,128,4,128]{3,2,1,0:T(4,128)(2,1)}), bf16[32,128,4,128]{3,2,1,0:T(4,128)(2,1)}, u32[]{:S(2)}, u32[]{:S(2)}) %all-to-all-start.2) | async-done | bytes 4194336 | tf_op jit(solution)/shard_map/all_to_all | solution.py:182
  663.3 4.6 fusion.10
  673.6 53.2 %while.27 = (s32[]{:T(128)}, f32[4,128,128]{2,1,0:T(8,128)S(1)}, s32[]{:T(128)}, f32[32,4]{1,0:T(8,128)}, f32[32,4,128,128]{3,2,1,0:T(8,128)}, /*index=5*/s32[]{:T(128)}, s32[]{:T(128)}, s32[]{:T(128)}, s32[]{:T(128)}) while((s32[]{:T(128)}, f32[4,128,128]{2,1,0:T(8,128)S(1)}, s32[]{:T(128)}, f32[32,4]{1,0:T(8,128)}, ...), condition=%wide.region_12.14_spmd, body=%wide.region_11.13_spmd.sunk | while | flops 131078 | bytes 786635 | solution.py:25
  674.3 1.1 bitcast_add_fusion.5
  676.1 1.1 bitcast_add_fusion.5
  677.9 1.1 bitcast_add_fusion.5
  679.7 1.1 bitcast_add_fusion.5
  681.4 1.1 bitcast_add_fusion.5
  683.2 1.1 bitcast_add_fusion.5
  685.0 1.1 bitcast_add_fusion.5
  686.7 1.1 bitcast_add_fusion.5
  690.3 1.1 bitcast_add_fusion.5
  692.1 1.1 bitcast_add_fusion.5
  (167 shorter events, 65.0 us)
Async XLA Ops:
  7.2 217.2 %copy-start = (bf16[128,4,128]{2,1,0:T(4,128)(2,1)S(1)}, bf16[128,4,128]{2,1,0:T(4,128)(2,1)}, u32[]{:S(2)}) copy-start(bf16[128,4,128]{2,1,0:T(4,128)(2,1)} %param.22) | copy-start | bytes 393220
  7.2 87.6 %all-gather.10.cloned.1.call-start = ((), (), s32[]{:S(2)}) async-start(), calls=%async_computation.4 | async-start | bytes 4325376 | tf_op jit(solution)/shard_map/all_gather | solution.py:139
  7.9 168.1 %all-gather.8.cloned.1.call-start = ((), (), s32[]{:S(2)}) async-start(), calls=%async_computation.3 | async-start | bytes 4325376 | tf_op jit(solution)/shard_map/all_gather | solution.py:138
  8.7 435.1 %all-gather.12.cloned.1.call-start = ((), (), s32[]{:S(2)}) async-start(), calls=%async_computation.5 | async-start | bytes 8650752 | tf_op jit(solution)/shard_map/all_gather | solution.py:16
  9.7 432.2 %copy-start.15 = (f32[4,128]{1,0:T(4,128)}, f32[4,128]{1,0:T(4,128)S(1)}, u32[]{:S(2)}) copy-start(f32[4,128]{1,0:T(4,128)S(1)} %reduce_window_sum.11) | copy-start | bytes 6148
  10.5 0.6 copy-start.17
  14.5 230.9 %all-to-all-start = ((s32[32,1,16]{2,1,0:T(1,128)}), s32[32,1,16]{2,1,0:T(1,128)S(1)}, u32[]{:S(2)}, u32[]{:S(2)}) async-start(s32[32,1,16]{2,1,0:T(1,128)} %stack.2), calls=%async_computation | async-start | bytes 32768 | tf_op jit(solution)/shard_map/all_to_all | solution.py:118
  26.8 197.5 %copy-start.13 = (bf16[128,4,128]{2,0,1:T(8,128)(2,1)}, bf16[128,4,128]{2,0,1:T(8,128)(2,1)S(1)}, u32[]{:S(2)}) copy-start(bf16[128,4,128]{2,0,1:T(8,128)(2,1)S(1)} %copy.404) | copy-start | bytes 393220
  27.5 206.2 %copy-start.23 = (pred[16]{0:T(512)(128)(4,1)}, pred[16]{0:T(512)(128)(4,1)S(1)}, u32[]{:S(2)}) copy-start(pred[16]{0:T(512)(128)(4,1)S(1)} %iota_compare_fusion.4) | copy-start | bytes 52
  224.3 3.9 copy-start.3
  228.2 2.7 copy-start.25
  228.2 2.7 copy-start.7
  231.6 2.0 copy-start.1
  231.7 2.0 copy-start.21
  245.4 6.7 copy-start.27
  245.4 196.6 %copy-start.5 = (bf16[128,4,128]{2,1,0:T(4,128)(2,1)S(1)}, bf16[128,4,128]{2,1,0:T(4,128)(2,1)}, u32[]{:S(2)}) copy-start(bf16[128,4,128]{2,1,0:T(4,128)(2,1)} %param.17) | copy-start | bytes 393220
  245.4 196.6 %copy-start.6 = (bf16[128,4,128]{2,1,0:T(4,128)(2,1)S(1)}, bf16[128,4,128]{2,1,0:T(4,128)(2,1)}, u32[]{:S(2)}) copy-start(bf16[128,4,128]{2,1,0:T(4,128)(2,1)} %param.18) | copy-start | bytes 393220
  245.4 196.8 %copy-start.4 = (bf16[128,4,128]{2,1,0:T(4,128)(2,1)S(1)}, bf16[128,4,128]{2,1,0:T(4,128)(2,1)}, u32[]{:S(2)}) copy-start(bf16[128,4,128]{2,1,0:T(4,128)(2,1)} %param.19) | copy-start | bytes 393220
  245.4 200.1 %all-to-all-start.1 = ((bf16[32,128,4,128]{3,2,1,0:T(4,128)(2,1)}), bf16[32,128,4,128]{3,2,1,0:T(4,128)(2,1)}, u32[]{:S(2)}, u32[]{:S(2)}) async-start(bf16[32,128,4,128]{3,2,1,0:T(4,128)(2,1)} %copy.264), calls=%async_computation.1 | async-start | bytes 8388608 | tf_op jit(solution)/shard_map/all_to_all | solution.py:183
  252.0 421.6 %all-gather.14.cloned.1.call-start = ((), (), s32[]{:S(2)}) async-start(), calls=%async_computation.6 | async-start | bytes 8650752 | tf_op jit(solution)/shard_map/all_gather | solution.py:16
  442.2 2.7 copy-start.9
  444.9 0.6 copy-start.20
  445.5 4.7 copy-start.11
  471.2 1.9 copy-start.8
  471.2 1.9 copy-start.26
  476.9 2.1 copy-start.2
  476.9 2.1 copy-start.22
  476.9 2.1 copy-start.24
  490.3 41.0 %copy-start.14 = (bf16[128,4,128]{2,0,1:T(8,128)(2,1)S(1)}, bf16[128,4,128]{2,0,1:T(8,128)(2,1)}, u32[]{:S(2)}) copy-start(bf16[128,4,128]{2,0,1:T(8,128)(2,1)} %copy-done.13) | copy-start | bytes 393220
  490.3 173.0 %all-to-all-start.2 = ((bf16[32,128,4,128]{3,2,1,0:T(4,128)(2,1)}), bf16[32,128,4,128]{3,2,1,0:T(4,128)(2,1)}, u32[]{:S(2)}, u32[]{:S(2)}) async-start(bf16[32,128,4,128]{3,2,1,0:T(4,128)(2,1)} %copy.301), calls=%async_computation.2 | async-start | bytes 8388608 | tf_op jit(solution)/shard_map/all_to_all | solution.py:182
  533.7 136.0 %copy-start.12 = (bf16[128,4,128]{2,0,1:T(8,128)(2,1)S(1)}, bf16[128,4,128]{2,0,1:T(8,128)(2,1)}, u32[]{:S(2)}) copy-start(bf16[128,4,128]{2,0,1:T(8,128)(2,1)} %get-tuple-element.199) | copy-start | bytes 393220
  533.7 136.7 %copy-start.16 = (f32[4,128]{1,0:T(4,128)S(1)}, f32[4,128]{1,0:T(4,128)}, u32[]{:S(2)}) copy-start(f32[4,128]{1,0:T(4,128)} %copy-done.15) | copy-start | bytes 6148
  533.8 137.4 %copy-start.19 = (f32[128,4]{0,1:T(4,128)S(1)}, f32[128,4]{0,1:T(4,128)}, u32[]{:S(2)}) copy-start(f32[128,4]{0,1:T(4,128)} %get-tuple-element.202) | copy-start | bytes 6148
  534.6 138.4 %copy-start.10 = (f32[4,128,128]{2,1,0:T(8,128)S(1)}, f32[4,128,128]{2,1,0:T(8,128)}, u32[]{:S(2)}) copy-start(f32[4,128,128]{2,1,0:T(8,128)} %copy-done.9) | copy-start | bytes 786436
  670.5 56.4 %copy-start.18 = (f32[128,4]{0,1:T(4,128)S(1)}, f32[128,4]{0,1:T(4,128)}, u32[]{:S(2)}) copy-start(f32[128,4]{0,1:T(4,128)} %copy-done.17) | copy-start | bytes 6148
Sparse Core Ops, SparseCore 0:
  10.6 84.1 all-gather.9
  97.4 78.5 all-gather.7
  178.6 148.6 all-gather.11
  468.5 195.7 all-gather.13
